TPU v7x, 512 devices: a whole 4x8x8 slice. The times are simulated.
512 devices in a mesh: depth: 64 (over z, y), strip: 8 (over x, core).
Axes of the slice: x: 4, y: 8, z: 8, core: 2. Of those that a mesh axis runs over, the one named last changes fastest.
Arguments:
- volume: float32 [128, 512, 1024], P('strip', 'depth'), may hold values from -4.5 to 6.5
- extinction: float32 [1], replicated, may hold values from 0.0005859375 to 0.001953125
- color_map: float32 [3, 2], replicated, may hold values from -3 to 3
- light_direction: float32 [3], replicated, may hold values from -4 to 4
Outputs:
- image: float32 [4, 128, 1024], P(None, 'strip', 'depth')
All inputs are finite; a program needn't handle non-finite values.
Results may differ from a plain program's by a relative error of at most 0.000034.
Values sent between devices are 32-bit elements; how exact they have to be, the bound alone decides.
No kernel may reach another device: no remote copies, remote signals or barrier semaphores. Data moves between devices by JAX's collectives and lax.ppermute only.
A program may use at most 64 MiB of HBM per device.

v0:
```python
import jax
import jax.numpy as jnp
from jax import lax
from jax.sharding import PartitionSpec as P


def extended_2(block, sides, width):
    for axis, dim in sides:
        count = lax.axis_size(axis)
        forward = [(i, i + 1) for i in range(count - 1)]
        backward = [(target, source) for source, target in forward]
        low = lax.ppermute(
            lax.slice_in_dim(block, block.shape[dim] - width, None, axis=dim), axis, forward
        )
        high = lax.ppermute(lax.slice_in_dim(block, 0, width, axis=dim), axis, backward)
        block = jnp.concatenate([low, block, high], axis=dim)
    return block


def blur_valid(field_in, along):
    extent = field_in.shape[along]
    lower_cells = lax.slice_in_dim(field_in, 0, extent - 2, axis=along)
    middle = lax.slice_in_dim(field_in, 1, extent - 1, axis=along)
    upper_cells = lax.slice_in_dim(field_in, 2, extent, axis=along)
    return 0.25 * lower_cells + 0.5 * middle + 0.25 * upper_cells


def slope_valid(field_in, along):
    extent = field_in.shape[along]
    lower_cells = lax.slice_in_dim(field_in, 0, extent - 2, axis=along)
    upper_cells = lax.slice_in_dim(field_in, 2, extent, axis=along)
    return 0.5 * (upper_cells - lower_cells)


def smooth_all(padded):
    return blur_valid(blur_valid(blur_valid(padded, 0), 1), 2)


def gradients(padded):
    first = blur_valid(blur_valid(slope_valid(padded, 0), 1), 2)
    second = blur_valid(blur_valid(slope_valid(padded, 1), 0), 2)
    third = blur_valid(blur_valid(slope_valid(padded, 2), 0), 1)
    return (first, second, third)


def pad_columns(field_in):
    return jnp.pad(field_in, ((0, 0), (0, 0), (1, 1)))


def render_slab(smoothed, gradient, extinction, color_map, light_direction):
    facing = (
        gradient[0] * light_direction[0]
        + gradient[1] * light_direction[1]
        + gradient[2] * light_direction[2]
    )
    shading = 0.3 + 0.7 * facing * facing / (1.0 + facing * facing)
    optical = extinction[0] * jax.nn.softplus(2.0 * smoothed)
    opacity = 1.0 - jnp.exp(-optical)
    prior_depth = jnp.cumsum(optical, axis=1) - optical
    weights = jnp.exp(-prior_depth) * opacity * shading
    colors = jnp.stack(
        [
            jnp.sum(
                weights * jax.nn.sigmoid(color_map[channel, 0] * smoothed + color_map[channel, 1]),
                axis=1,
            )
            for channel in range(3)
        ],
        0,
    )
    transmit = jnp.exp(-jnp.sum(optical, axis=1))
    return jnp.concatenate([colors, transmit[None]], 0)


def local(volume, extinction, color_map, light_direction):
    row_count, slab_count, column_count = volume.shape
    groups = lax.axis_size("depth")
    extended = extended_2(volume, (("depth", 1), ("strip", 0)), 2)
    filtered = smooth_all(pad_columns(extended))
    row_global = lax.axis_index("strip") * row_count + jnp.arange(row_count + 2) - 1
    slab_global = lax.axis_index("depth") * slab_count + jnp.arange(slab_count + 2) - 1
    row_inside = (row_global >= 0) & (row_global < row_count * lax.axis_size("strip"))
    slab_inside = (slab_global >= 0) & (slab_global < slab_count * groups)
    inside = (row_inside[:, None] & slab_inside[None, :]).astype(jnp.float32)
    filtered = filtered * inside[:, :, None]
    smoothed = filtered[1:-1, 1:-1]
    gradient = gradients(pad_columns(filtered))
    partial_value = render_slab(smoothed, gradient, extinction, color_map, light_direction)
    layers = lax.all_to_all(
        partial_value[:, :, None, :], "depth", split_axis=3, concat_axis=2, tiled=True
    )
    through = jnp.cumprod(layers[3], axis=1)
    prior_pass = jnp.concatenate([jnp.ones_like(through[:, :1]), through[:, :-1]], 1)
    colors = jnp.sum(prior_pass[None] * layers[:3], axis=2)
    transmit = through[:, -1]
    return jnp.concatenate([colors, 1.0 - transmit[None]], 0)


def solution(mesh):
    in_specs = (P("strip", "depth", None), P(), P(), P())
    out_specs = P(None, "strip", "depth")
    return jax.shard_map(local, mesh=mesh, in_specs=in_specs, out_specs=out_specs, check_vma=False)
```

profile of v0, /device:TPU:3, one launch (start us, length us, event | category | flops | bytes accessed | tf_op | source)
XLA Modules:
  0.0 90.2 jit_solution(13778293491945401389)
XLA Ops:
  0.0 0.0 copy-start
  0.0 0.0 copy-start.1
  0.0 1.4 %fusion.38 = (f32[16,2,1024]{2,1,0:T(2,128)S(1)}, f32[16,2,1024]{2,1,0:T(2,128)S(1)}) fusion(f32[16,8,1024]{2,1,0:T(8,128)} %param.4), kind=kLoop, calls=%fused_computation.92 | loop fusion | bytes 524288 | tf_op jit(solution)/shard_map/slice | solution.py:13
  1.4 3.2 %collective-permute-start = (f32[16,2,1024]{2,1,0:T(2,128)S(1)}, f32[16,2,1024]{2,1,0:T(2,128)S(1)}, u32[]{:S(2)}, u32[]{:S(2)}) collective-permute-start(f32[16,2,1024]{2,1,0:T(2,128)S(1)} %get-tuple-element.12), channel_id=1, source_target_pairs={{0,8},{8,16},{16,24},{24,32},{32,40},{40,48},{48,56},{56,64},{64,7... | collective-permute-start | bytes 393224 | tf_op jit(solution)/shard_map/ppermute | solution.py:12
  4.6 1.3 %collective-permute-start.1 = (f32[16,2,1024]{2,1,0:T(2,128)S(1)}, f32[16,2,1024]{2,1,0:T(2,128)S(1)}, u32[]{:S(2)}, u32[]{:S(2)}) collective-permute-start(f32[16,2,1024]{2,1,0:T(2,128)S(1)} %get-tuple-element.13), channel_id=1, source_target_pairs={{8,0},{16,8},{24,16},{32,24},{40,32},{48,40},{56,48},{64,56},{72,6... | collective-permute-start | bytes 393224 | tf_op jit(solution)/shard_map/ppermute | solution.py:15
  5.9 0.1 and_convert_fusion
  6.7 1.6 %fusion.39 = (f32[1,1]{0,1:T(1,128)}, f32[1,1]{0,1:T(1,128)}, f32[1,1]{0,1:T(1,128)}, f32[1,1]{0,1:T(1,128)}, f32[1,1]{0,1:T(1,128)}, /*index=5*/f32[1,1]{0,1:T(1,128)}) fusion(f32[3,2]{0,1:T(2,128)} %param.6), kind=kLoop, calls=%fused_computation.93 | loop fusion | bytes 48 | tf_op jit(solution)/shard_map/slice | solution.py:64
  8.2 0.0 collective-permute-done
  8.2 2.1 %collective-permute-done.1 = f32[16,2,1024]{2,1,0:T(2,128)S(1)} collective-permute-done((f32[16,2,1024]{2,1,0:T(2,128)S(1)}, f32[16,2,1024]{2,1,0:T(2,128)S(1)}, u32[]{:S(2)}, u32[]{:S(2)}) %collective-permute-start.1) | collective-permute-done | bytes 131104 | tf_op jit(solution)/shard_map/ppermute | solution.py:15
  10.3 0.9 %pad_maximum_fusion.3 = (f32[2,12,1024]{2,1,0:T(8,128)S(1)}, f32[2,12,1024]{2,1,0:T(8,128)S(1)}) fusion(f32[16,2,1024]{2,1,0:T(2,128)S(1)} %collective-permute-done.1, f32[16,8,1024]{2,1,0:T(8,128)} %param.4, f32[16,2,1024]{2,1,0:T(2,128)S(1)} %collective-permute-done), kind=kLoop, calls=%fused_computation.83 | loop fusion | flops 98304 | bytes 983040 | tf_op jit(solution)/shard_map/slice | solution.py:13
  11.2 5.1 %collective-permute-start.2 = (f32[2,12,1024]{2,1,0:T(8,128)S(1)}, f32[2,12,1024]{2,1,0:T(8,128)S(1)}, u32[]{:S(2)}, u32[]{:S(2)}) collective-permute-start(f32[2,12,1024]{2,1,0:T(8,128)S(1)} %get-tuple-element.10), channel_id=1, source_target_pairs={{0,1},{1,2},{2,3},{3,4},{4,5},{5,6},{6,7},{8,9},{9,10},{10,11},{11... | collective-permute-start | bytes 294920 | tf_op jit(solution)/shard_map/ppermute | solution.py:12
  16.3 1.9 %collective-permute-start.3 = (f32[2,12,1024]{2,1,0:T(8,128)S(1)}, f32[2,12,1024]{2,1,0:T(8,128)S(1)}, u32[]{:S(2)}, u32[]{:S(2)}) collective-permute-start(f32[2,12,1024]{2,1,0:T(8,128)S(1)} %get-tuple-element.11), channel_id=1, source_target_pairs={{1,0},{2,1},{3,2},{4,3},{5,4},{6,5},{7,6},{9,8},{10,9},{11,10},{12... | collective-permute-start | bytes 294920 | tf_op jit(solution)/shard_map/ppermute | solution.py:15
  18.3 0.0 copy-done.1
  18.3 0.6 fusion.40
  18.9 0.0 collective-permute-done.2
  18.9 3.7 %collective-permute-done.3 = f32[2,12,1024]{2,1,0:T(8,128)S(1)} collective-permute-done((f32[2,12,1024]{2,1,0:T(8,128)S(1)}, f32[2,12,1024]{2,1,0:T(8,128)S(1)}, u32[]{:S(2)}, u32[]{:S(2)}) %collective-permute-start.3) | collective-permute-done | bytes 98336 | tf_op jit(solution)/shard_map/ppermute | solution.py:15
  22.6 0.0 copy-done
  22.6 0.8 select_maximum_fusion
  23.4 0.2 fusion.3
  23.6 0.4 fusion.1
  24.0 0.7 fusion.10
  24.7 0.7 fusion.6
  25.4 0.4 fusion.15
  25.8 0.7 fusion.8
  26.5 1.1 %fusion.36 = (f32[16,1024]{1,0:T(8,128)S(1)}, f32[16,8,1024]{2,1,0:T(8,128)}) fusion(f32[18,10,1024]{2,1,0:T(8,128)S(1)} %fusion.10, f32[]{:T(128)} %bitcast.26), kind=kLoop, calls=%fused_computation.91 | loop fusion | flops 1163264 | bytes 1114116 | tf_op jit(solution)/shard_map/reduce_sum | solution.py:71
  27.6 0.2 fusion.12
  27.9 0.3 fusion.16
  28.1 2.3 %reduce_window_sum.11 = f32[16,8,1024]{2,1,0:T(8,128)} reduce-window(f32[16,8,1024]{2,1,0:T(8,128)} %get-tuple-element.9, f32[]{:T(128)} %constant.16.clone.1), window={size=1x8x1 pad=0_0x7_0x0_0}, to_apply=%region_0.1 | reduce-window | flops 917504 | bytes 1048580 | tf_op jit(solution)/shard_map/jit(cumsum)/reduce_window_sum | solution.py:59
  30.4 8.3 %multiply_reduce_fusion.3 = (f32[16,1024]{1,0:T(8,128)S(1)}, f32[16,1024]{1,0:T(8,128)S(1)}, f32[16,1024]{1,0:T(8,128)S(1)}) fusion(f32[18,10,1024]{2,1,0:T(8,128)S(1)} %fusion.10, f32[]{:T(128)} %bitcast.5, f32[]{:T(128)} %bitcast.4, f32[]{:T(128)} %bitcast.11, f32[]{:T(128)} %bitcast.10, f32[]{:T(128)} %bitcast.8, f32[]{:T(128)} %bitcast.7, f32[]{:T(128)} %bitcast.3, ...), kind=kLoop, calls=%fused_computation.79 | loop fusion | flops 6897664 | bytes 6488100 | tf_op jit(solution)/shard_map/reduce_sum | solution.py:63
  38.8 0.8 copy.12
  39.6 1.5 %bitcast_bitcast_fusion = f32[1024,1,4,16]{3,2,1,0:T(4,128)} fusion(f32[4,16,1024]{1,0,2:T(4,128)S(1)} %copy.12), kind=kLoop, calls=%fused_computation.95 | loop fusion | bytes 524288
  41.1 3.2 %reshape.83 = f32[64,1,1024]{2,1,0:T(1,128)S(1)} reshape(f32[1024,1,4,16]{3,2,1,0:T(4,128)} %bitcast_bitcast_fusion) | data formatting | bytes 524288
  44.3 30.7 %all_to_all.4 = f32[64,1,1024]{2,1,0:T(1,128)S(1)} all-to-all(f32[64,1,1024]{2,1,0:T(1,128)S(1)} %reshape.83), channel_id=1, replica_groups=mesh['depth'=64,'strip'=8] {'depth'}, dimensions={0} | all-to-all | bytes 524288 | tf_op jit(solution)/shard_map/all_to_all | solution.py:89
  75.0 0.5 broadcast.177
  75.5 1.3 %reduce = f32[64,1024]{1,0:T(8,128)S(1)} reduce(f32[64,1,1024]{2,1,0:T(1,128)S(1)} %all_to_all.4, f32[]{:T(128)} %broadcast.177), dimensions={1}, to_apply=%all_to_all.2.reduce_sub_computation | reduce | bytes 524292 | tf_op jit(solution)/shard_map/all_to_all | solution.py:89
  76.8 1.5 %reshape.84 = f32[1024,1,4,16]{3,2,1,0:T(4,128)S(1)} reshape(f32[64,1024]{1,0:T(8,128)S(1)} %reduce) | data formatting | bytes 524288
  78.3 0.5 slice.238
  78.8 0.2 copy.14
  79.0 6.3 %fusion.41 = f32[16,64,16]{2,0,1:T(8,128)S(1)} fusion(f32[16,64,16]{2,0,1:T(8,128)S(1)} %copy.14), kind=kOutput, calls=%fused_computation.96 | output fusion | flops 1032192 | bytes 131072 | tf_op jit(solution)/shard_map/jit(cumprod)/reduce_window | solution.py:92
  85.4 0.2 copy.20
  85.6 2.2 %copy.19 = f32[3,16,64,16]{3,2,1,0:T(8,128)} copy(f32[3,16,64,16]{1,0,3,2:T(4,128)S(1)} %bitcast.28) | data formatting | bytes 393216 | tf_op jit(solution)/shard_map/slice | solution.py:94
  87.8 0.1 concatenate.18.clone
  87.9 1.7 %multiply_reduce_fusion = f32[3,16,16]{2,1,0:T(8,128)S(1)} fusion(f32[3,16,64,16]{3,2,1,0:T(8,128)} %copy.19, f32[16,64,16]{2,1,0:T(8,128)S(1)} %concatenate.18.clone), kind=kLoop, calls=%fused_computation.2 | loop fusion | flops 97536 | bytes 265216 | tf_op jit(solution)/shard_map/reduce_sum | solution.py:94
  89.6 0.6 pad_maximum_fusion.4
  (6 shorter events, 0.1 us)
Async XLA Ops:
  0.0 22.6 %copy-start = (f32[16,8,1024]{2,1,0:T(8,128)S(1)}, f32[16,8,1024]{2,1,0:T(8,128)}, u32[]{:S(2)}) copy-start(f32[16,8,1024]{2,1,0:T(8,128)} %param.4) | copy-start | bytes 1572868
  0.0 18.3 %copy-start.1 = (f32[3]{0:T(128)S(1)}, f32[3]{0:T(128)}, u32[]{:S(2)}) copy-start(f32[3]{0:T(128)} %param.7) | copy-start | bytes 40
  1.4 6.9 %collective-permute-start = (f32[16,2,1024]{2,1,0:T(2,128)S(1)}, f32[16,2,1024]{2,1,0:T(2,128)S(1)}, u32[]{:S(2)}, u32[]{:S(2)}) collective-permute-start(f32[16,2,1024]{2,1,0:T(2,128)S(1)} %get-tuple-element.12), channel_id=1, source_target_pairs={{0,8},{8,16},{16,24},{24,32},{32,40},{40,48},{48,56},{56,64},{64,7... | collective-permute-start | bytes 393224 | tf_op jit(solution)/shard_map/ppermute | solution.py:12
  4.6 5.7 %collective-permute-start.1 = (f32[16,2,1024]{2,1,0:T(2,128)S(1)}, f32[16,2,1024]{2,1,0:T(2,128)S(1)}, u32[]{:S(2)}, u32[]{:S(2)}) collective-permute-start(f32[16,2,1024]{2,1,0:T(2,128)S(1)} %get-tuple-element.13), channel_id=1, source_target_pairs={{8,0},{16,8},{24,16},{32,24},{40,32},{48,40},{56,48},{64,56},{72,6... | collective-permute-start | bytes 393224 | tf_op jit(solution)/shard_map/ppermute | solution.py:15
  11.2 7.7 %collective-permute-start.2 = (f32[2,12,1024]{2,1,0:T(8,128)S(1)}, f32[2,12,1024]{2,1,0:T(8,128)S(1)}, u32[]{:S(2)}, u32[]{:S(2)}) collective-permute-start(f32[2,12,1024]{2,1,0:T(8,128)S(1)} %get-tuple-element.10), channel_id=1, source_target_pairs={{0,1},{1,2},{2,3},{3,4},{4,5},{5,6},{6,7},{8,9},{9,10},{10,11},{11... | collective-permute-start | bytes 294920 | tf_op jit(solution)/shard_map/ppermute | solution.py:12
  16.3 6.3 %collective-permute-start.3 = (f32[2,12,1024]{2,1,0:T(8,128)S(1)}, f32[2,12,1024]{2,1,0:T(8,128)S(1)}, u32[]{:S(2)}, u32[]{:S(2)}) collective-permute-start(f32[2,12,1024]{2,1,0:T(8,128)S(1)} %get-tuple-element.11), channel_id=1, source_target_pairs={{1,0},{2,1},{3,2},{4,3},{5,4},{6,5},{7,6},{9,8},{10,9},{11,10},{12... | collective-permute-start | bytes 294920 | tf_op jit(solution)/shard_map/ppermute | solution.py:15
where the time goes:
time: 90.7 us; the launch traced here: 90.2 us
  blocking collectives  30.7 us (34%)
  other arithmetic  27 us (30%)
  local copies, waits for them, and re-layouts  14.3 us (16%)
  starting transfers between devices  11.5 us (13%)
  waiting for transfers between devices  5.76 us (6%)
    all_to_all x1, blocking collectives, local(): lax.all_to_all(partial_value[:, :, None, :], 'depth', split_axis=3, conca...  30.7 us
    reduce_sum x1, other arithmetic, render_slab(): jnp.sum(weights * jax.nn.sigmoid(color_map[channel, 0] * smoothed + color...  8.34 us
    ppermute x2, starting transfers between devices, extended_2(): lax.ppermute(lax.slice_in_dim(block, block.shape[dim] - width, None, axis...  8.32 us
    unnamed x8, local copies, waits for them, and re-layouts  6.35 us
    another operation x1, other arithmetic, local(): through = jnp.cumprod(layers[3], axis=1)  6.33 us
    ppermute x2, waiting for transfers between devices, extended_2(): lax.ppermute(lax.slice_in_dim(block, 0, width, axis=dim), axis, backward)  5.76 us
    ppermute x2, starting transfers between devices, extended_2(): lax.ppermute(lax.slice_in_dim(block, 0, width, axis=dim), axis, backward)  3.21 us
    another operation x1, other arithmetic, render_slab(): prior_depth = jnp.cumsum(optical, axis=1) - optical  2.28 us
  transfers between devices with their start and end apart: 4, of which 2 were waited for; matrix products, arithmetic and copies ran while one was open for 3% of the time, Pallas kernels for 0%

commit v1 on v0

--- a/solution.py
+++ b/solution.py
@@ -2,6 +2,19 @@
 import jax.numpy as jnp
 from jax import lax
 from jax.sharding import PartitionSpec as P
+
+
+def build_stocks(s0):
+    lower = jnp.concatenate(
+        lax.all_to_all(
+            jnp.stack(jnp.split(s0, lax.axis_size("depth"), 3), 0),
+            axis_name="depth",
+            split_axis=0,
+            concat_axis=0,
+        ),
+        2,
+    )
+    return lower
 
 
 def extended_2(block, sides, width):
@@ -86,9 +99,7 @@
     smoothed = filtered[1:-1, 1:-1]
     gradient = gradients(pad_columns(filtered))
     partial_value = render_slab(smoothed, gradient, extinction, color_map, light_direction)
-    layers = lax.all_to_all(
-        partial_value[:, :, None, :], "depth", split_axis=3, concat_axis=2, tiled=True
-    )
+    layers = build_stocks(partial_value[:, :, None, :])
     through = jnp.cumprod(layers[3], axis=1)
     prior_pass = jnp.concatenate([jnp.ones_like(through[:, :1]), through[:, :-1]], 1)
     colors = jnp.sum(prior_pass[None] * layers[:3], axis=2)

time: 90.7 us -> 80.2 us (0.88)
  other arithmetic: 27 us -> 20.4 us
  local copies, waits for them, and re-layouts: 14.3 us -> 11.1 us
    another operation x1, other arithmetic: 6.33 us -> 0.07 us  [local(): through = jnp.cumprod(layers[3], axis=1)]
    slice x2 -> x0, local copies, waits for them, and re-layouts: 2.76 us -> none  [the longest x1 2.21 us: local(): colors = jnp.sum(prior_pass[None] * layers[:3], axis=2)]
    reduce_sum x1, other arithmetic: 1.7 us -> 0.27 us  [local(): colors = jnp.sum(prior_pass[None] * layers[:3], axis=2)]
    concatenate x1, other arithmetic: 0.76 us -> 1.84 us  [extended_2(): block = jnp.concatenate([low, block, high], axis=dim)]
    unnamed x8 -> x66, local copies, waits for them, and re-layouts: 6.35 us -> 5.87 us
  transfers between devices with their start and end apart: 4 -> 4, of which waited for: 2 -> 2; matrix products, arithmetic and copies ran while one was open for 3% -> 4% of each run, Pallas kernels for 0% -> 0%
where the time goes in v1:
time: 80.2 us; the launch traced here: 79.6 us
  blocking collectives  30.7 us (38%)
  other arithmetic  20.4 us (25%)
  starting transfers between devices  11.5 us (14%)
  local copies, waits for them, and re-layouts  11.1 us (14%)
  waiting for transfers between devices  5.01 us (6%)
  between operations  0.95 us (1%)
    all_to_all x1, blocking collectives, build_stocks(): lax.all_to_all(jnp.stack(jnp.split(s0, lax.axis_size('depth'), 3), 0), ax...  30.7 us
    reduce_sum x1, other arithmetic, render_slab(): jnp.sum(weights * jax.nn.sigmoid(color_map[channel, 0] * smoothed + color...  8.34 us
    ppermute x2, starting transfers between devices, extended_2(): lax.ppermute(lax.slice_in_dim(block, block.shape[dim] - width, None, axis...  8.32 us
    unnamed x66, local copies, waits for them, and re-layouts  5.87 us
    ppermute x2, waiting for transfers between devices, extended_2(): lax.ppermute(lax.slice_in_dim(block, 0, width, axis=dim), axis, backward)  5 us
    ppermute x2, starting transfers between devices, extended_2(): lax.ppermute(lax.slice_in_dim(block, 0, width, axis=dim), axis, backward)  3.21 us
    another operation x1, other arithmetic, render_slab(): prior_depth = jnp.cumsum(optical, axis=1) - optical  2.28 us
    concatenate x1, other arithmetic, extended_2(): block = jnp.concatenate([low, block, high], axis=dim)  1.84 us
  transfers between devices with their start and end apart: 4, of which 2 were waited for; matrix products, arithmetic and copies ran while one was open for 4% of the time, Pallas kernels for 0%

profile of v1, /device:TPU:3, one launch (start us, length us, event | category | flops | bytes accessed | tf_op | source)
XLA Modules:
  0.0 79.6 jit_solution(1532458380561240820)
XLA Ops:
  0.0 1.4 %fusion.41 = (f32[16,2,1024]{2,1,0:T(2,128)S(1)}, f32[16,2,1024]{2,1,0:T(2,128)S(1)}) fusion(f32[16,8,1024]{2,1,0:T(8,128)} %param.4), kind=kLoop, calls=%fused_computation.224 | loop fusion | bytes 524288 | tf_op jit(solution)/shard_map/slice | solution.py:26
  1.4 3.2 %collective-permute-start = (f32[16,2,1024]{2,1,0:T(2,128)S(1)}, f32[16,2,1024]{2,1,0:T(2,128)S(1)}, u32[]{:S(2)}, u32[]{:S(2)}) collective-permute-start(f32[16,2,1024]{2,1,0:T(2,128)S(1)} %get-tuple-element.12), channel_id=1, source_target_pairs={{0,8},{8,16},{16,24},{24,32},{32,40},{40,48},{48,56},{56,64},{64,7... | collective-permute-start | bytes 393224 | tf_op jit(solution)/shard_map/ppermute | solution.py:25
  4.6 1.3 %collective-permute-start.1 = (f32[16,2,1024]{2,1,0:T(2,128)S(1)}, f32[16,2,1024]{2,1,0:T(2,128)S(1)}, u32[]{:S(2)}, u32[]{:S(2)}) collective-permute-start(f32[16,2,1024]{2,1,0:T(2,128)S(1)} %get-tuple-element.13), channel_id=1, source_target_pairs={{8,0},{16,8},{24,16},{32,24},{40,32},{48,40},{56,48},{64,56},{72,6... | collective-permute-start | bytes 393224 | tf_op jit(solution)/shard_map/ppermute | solution.py:28
  6.7 1.6 %fusion.42 = (f32[1,1]{0,1:T(1,128)}, f32[1,1]{0,1:T(1,128)}, f32[1,1]{0,1:T(1,128)}, f32[1,1]{0,1:T(1,128)}, f32[1,1]{0,1:T(1,128)}, /*index=5*/f32[1,1]{0,1:T(1,128)}) fusion(f32[3,2]{0,1:T(2,128)} %param.6), kind=kLoop, calls=%fused_computation.225 | loop fusion | bytes 48 | tf_op jit(solution)/shard_map/slice | solution.py:77
  8.3 2.1 %collective-permute-done.1 = f32[16,2,1024]{2,1,0:T(2,128)S(1)} collective-permute-done((f32[16,2,1024]{2,1,0:T(2,128)S(1)}, f32[16,2,1024]{2,1,0:T(2,128)S(1)}, u32[]{:S(2)}, u32[]{:S(2)}) %collective-permute-start.1) | collective-permute-done | bytes 131104 | tf_op jit(solution)/shard_map/ppermute | solution.py:28
  10.3 0.9 %pad_maximum_fusion.2 = (f32[2,12,1024]{2,1,0:T(8,128)S(1)}, f32[2,12,1024]{2,1,0:T(8,128)S(1)}) fusion(f32[16,2,1024]{2,1,0:T(2,128)S(1)} %collective-permute-done.1, f32[16,8,1024]{2,1,0:T(8,128)} %param.4, f32[16,2,1024]{2,1,0:T(2,128)S(1)} %collective-permute-done), kind=kLoop, calls=%fused_computation.151 | loop fusion | flops 98304 | bytes 983040 | tf_op jit(solution)/shard_map/slice | solution.py:26
  11.3 5.1 %collective-permute-start.2 = (f32[2,12,1024]{2,1,0:T(8,128)S(1)}, f32[2,12,1024]{2,1,0:T(8,128)S(1)}, u32[]{:S(2)}, u32[]{:S(2)}) collective-permute-start(f32[2,12,1024]{2,1,0:T(8,128)S(1)} %get-tuple-element.10), channel_id=1, source_target_pairs={{0,1},{1,2},{2,3},{3,4},{4,5},{5,6},{6,7},{8,9},{9,10},{10,11},{11... | collective-permute-start | bytes 294920 | tf_op jit(solution)/shard_map/ppermute | solution.py:25
  16.4 1.9 %collective-permute-start.3 = (f32[2,12,1024]{2,1,0:T(8,128)S(1)}, f32[2,12,1024]{2,1,0:T(8,128)S(1)}, u32[]{:S(2)}, u32[]{:S(2)}) collective-permute-start(f32[2,12,1024]{2,1,0:T(8,128)S(1)} %get-tuple-element.11), channel_id=1, source_target_pairs={{1,0},{2,1},{3,2},{4,3},{5,4},{6,5},{7,6},{9,8},{10,9},{11,10},{12... | collective-permute-start | bytes 294920 | tf_op jit(solution)/shard_map/ppermute | solution.py:28
  18.3 1.4 %fusion.43 = (f32[1]{0:T(128)}, f32[1]{0:T(128)}, f32[1]{0:T(128)}) fusion(f32[3]{0:T(128)} %param.7), kind=kLoop, calls=%fused_computation.226 | loop fusion | bytes 24 | tf_op jit(solution)/shard_map/slice | solution.py:65
  19.7 2.9 %collective-permute-done.3 = f32[2,12,1024]{2,1,0:T(8,128)S(1)} collective-permute-done((f32[2,12,1024]{2,1,0:T(8,128)S(1)}, f32[2,12,1024]{2,1,0:T(8,128)S(1)}, u32[]{:S(2)}, u32[]{:S(2)}) %collective-permute-start.3) | collective-permute-done | bytes 98336 | tf_op jit(solution)/shard_map/ppermute | solution.py:28
  22.7 1.8 %select_maximum_fusion = f32[20,12,1026]{2,1,0:T(8,128)S(1)} fusion(f32[2,12,1024]{2,1,0:T(8,128)S(1)} %collective-permute-done.3, f32[2,12,1024]{2,1,0:T(8,128)S(1)} %collective-permute-done.2, f32[16,2,1024]{2,1,0:T(2,128)S(1)} %collective-permute-done.1, f32[16,8,1024]{2,1,0:T(8,128)} %param.4, f32[16,2,1024]{2,1,0:T(2,128)S(1)} %collective-permute-done), kind=kLoop, calls=%fused_computation.6 | loop fusion | flops 2954880 | bytes 1968000 | tf_op jit(solution)/shard_map/concatenate | solution.py:29
  24.5 0.2 fusion.5
  24.7 0.4 fusion.3
  25.1 0.7 fusion.12
  25.8 0.7 fusion.8
  26.5 0.4 fusion.17
  26.9 0.7 fusion.10
  27.6 1.1 %fusion.39 = (f32[16,1024]{1,0:T(8,128)S(1)}, f32[16,8,1024]{2,1,0:T(8,128)}) fusion(f32[18,10,1024]{2,1,0:T(8,128)S(1)} %fusion.12, f32[]{:T(128)} %bitcast.292), kind=kLoop, calls=%fused_computation.223 | loop fusion | flops 1163264 | bytes 1114116 | tf_op jit(solution)/shard_map/reduce_sum | solution.py:84
  28.7 0.2 fusion.14
  29.0 0.3 fusion.18
  29.3 2.3 %reduce_window_sum.11 = f32[16,8,1024]{2,1,0:T(8,128)} reduce-window(f32[16,8,1024]{2,1,0:T(8,128)} %get-tuple-element.9, f32[]{:T(128)} %constant.16.clone.1), window={size=1x8x1 pad=0_0x7_0x0_0}, to_apply=%region_0.1 | reduce-window | flops 917504 | bytes 1048580 | tf_op jit(solution)/shard_map/jit(cumsum)/reduce_window_sum | solution.py:72
  31.5 8.3 %multiply_reduce_fusion.2 = (f32[16,1024]{1,0:T(8,128)S(1)}, f32[16,1024]{1,0:T(8,128)S(1)}, f32[16,1024]{1,0:T(8,128)S(1)}) fusion(f32[18,10,1024]{2,1,0:T(8,128)S(1)} %fusion.12, f32[]{:T(128)} %bitcast.5, f32[]{:T(128)} %bitcast.4, f32[]{:T(128)} %bitcast.11, f32[]{:T(128)} %bitcast.10, f32[]{:T(128)} %bitcast.8, f32[]{:T(128)} %bitcast.7, f32[]{:T(128)} %bitcast.3, ...), kind=kLoop, calls=%fused_computation.83 | loop fusion | flops 6897664 | bytes 6488100 | tf_op jit(solution)/shard_map/reduce_sum | solution.py:76
  40.7 0.1 constant_dynamic-update-slice_fusion.51
  40.8 0.1 constant_dynamic-update-slice_fusion.50
  40.8 0.1 constant_dynamic-update-slice_fusion.49
  40.9 0.1 constant_dynamic-update-slice_fusion.48
  41.2 0.1 constant_dynamic-update-slice_fusion.43
  41.8 0.1 constant_dynamic-update-slice_fusion.35
  41.9 0.1 constant_dynamic-update-slice_fusion.34
  42.0 0.1 constant_dynamic-update-slice_fusion.33
  42.0 0.1 constant_dynamic-update-slice_fusion.32
  42.4 0.1 constant_dynamic-update-slice_fusion.27
  42.4 0.1 constant_dynamic-update-slice_fusion.26
  42.9 0.1 constant_dynamic-update-slice_fusion.19
  43.0 0.1 constant_dynamic-update-slice_fusion.18
  43.1 0.1 constant_dynamic-update-slice_fusion.17
  43.1 0.1 constant_dynamic-update-slice_fusion.16
  43.5 0.1 constant_dynamic-update-slice_fusion.11
  43.5 0.1 constant_dynamic-update-slice_fusion.10
  44.3 0.1 bitcast_bitcast_fusion.1
  44.5 0.7 reshape.79
  45.2 30.7 %all_to_all.5 = f32[64,1,1024]{2,1,0:T(1,128)S(1)} all-to-all(f32[64,1,1024]{2,1,0:T(1,128)S(1)} %reshape.79), channel_id=1, replica_groups=mesh['depth'=64,'strip'=8] {'depth'}, dimensions={0} | all-to-all | bytes 524288 | tf_op jit(solution)/shard_map/all_to_all | solution.py:9
  75.9 0.5 broadcast.173
  76.4 1.3 %reduce = f32[64,1024]{1,0:T(8,128)S(1)} reduce(f32[64,1,1024]{2,1,0:T(1,128)S(1)} %all_to_all.5, f32[]{:T(128)} %broadcast.173), dimensions={1}, to_apply=%all_to_all.3.reduce_sub_computation | reduce | bytes 524292 | tf_op jit(solution)/shard_map/all_to_all | solution.py:9
  77.7 0.7 reshape.80
  78.4 0.1 bitcast_bitcast_fusion
  78.7 0.3 fusion.1
  79.0 0.6 pad_maximum_fusion.3
  (58 shorter events, 3.3 us)
Async XLA Ops:
  1.4 6.9 %collective-permute-start = (f32[16,2,1024]{2,1,0:T(2,128)S(1)}, f32[16,2,1024]{2,1,0:T(2,128)S(1)}, u32[]{:S(2)}, u32[]{:S(2)}) collective-permute-start(f32[16,2,1024]{2,1,0:T(2,128)S(1)} %get-tuple-element.12), channel_id=1, source_target_pairs={{0,8},{8,16},{16,24},{24,32},{32,40},{40,48},{48,56},{56,64},{64,7... | collective-permute-start | bytes 393224 | tf_op jit(solution)/shard_map/ppermute | solution.py:25
  4.6 5.7 %collective-permute-start.1 = (f32[16,2,1024]{2,1,0:T(2,128)S(1)}, f32[16,2,1024]{2,1,0:T(2,128)S(1)}, u32[]{:S(2)}, u32[]{:S(2)}) collective-permute-start(f32[16,2,1024]{2,1,0:T(2,128)S(1)} %get-tuple-element.13), channel_id=1, source_target_pairs={{8,0},{16,8},{24,16},{32,24},{40,32},{48,40},{56,48},{64,56},{72,6... | collective-permute-start | bytes 393224 | tf_op jit(solution)/shard_map/ppermute | solution.py:28
  11.3 8.5 %collective-permute-start.2 = (f32[2,12,1024]{2,1,0:T(8,128)S(1)}, f32[2,12,1024]{2,1,0:T(8,128)S(1)}, u32[]{:S(2)}, u32[]{:S(2)}) collective-permute-start(f32[2,12,1024]{2,1,0:T(8,128)S(1)} %get-tuple-element.10), channel_id=1, source_target_pairs={{0,1},{1,2},{2,3},{3,4},{4,5},{5,6},{6,7},{8,9},{9,10},{10,11},{11... | collective-permute-start | bytes 294920 | tf_op jit(solution)/shard_map/ppermute | solution.py:25
  16.4 6.3 %collective-permute-start.3 = (f32[2,12,1024]{2,1,0:T(8,128)S(1)}, f32[2,12,1024]{2,1,0:T(8,128)S(1)}, u32[]{:S(2)}, u32[]{:S(2)}) collective-permute-start(f32[2,12,1024]{2,1,0:T(8,128)S(1)} %get-tuple-element.11), channel_id=1, source_target_pairs={{1,0},{2,1},{3,2},{4,3},{5,4},{6,5},{7,6},{9,8},{10,9},{11,10},{12... | collective-permute-start | bytes 294920 | tf_op jit(solution)/shard_map/ppermute | solution.py:28
